TPU v7x, 256 devices: a whole 4x4x8 slice. The times are simulated.
256 devices in a mesh: dp: 16 (over x, y_lo, core), fsdp: 16 (over z, y_hi).
Axes of the slice: x: 4, y: 4 (y_hi: 2, y_lo: 2; y = y_hi * 2 + y_lo), z: 8, core: 2. Of those that a mesh axis runs over, the one named last changes fastest.
Arguments:
- fields: bfloat16 [16, 6, 48, 48, 48, 128], P('dp', None, 'fsdp'), may hold values from -6 to 6
- targets: bfloat16 [16, 6, 48, 2304], P('dp', None, 'fsdp'), may hold values from -6 to 6
- lists: int32 [16, 6], P('dp'), may hold values from 0 to 5, each once within a row
- counts: int32 [16], replicated, may hold values from 1 to 6, as said below
- spectral_w: bfloat16 [32, 2, 128, 128], P('fsdp'), may hold values from -0.375 to 0.375
- local_w: bfloat16 [128, 128], replicated, may hold values from -0.5 to 0.5
- proj: float32 [128], replicated, may hold values from -0.5 to 0.5
Outputs:
- grad_spectral: float32 [32, 2, 128, 128], P('fsdp')
- grad_local: float32 [128, 128], replicated
Inputs may be any that keep to these rules, and one draw needn't show every extreme that they name: Each row of lists names every slot of its lane once; the first counts[l] entries of row l are lane l's live grids. `counts`: exactly one lane has 6 live grids; every other lane has 1 or 2.
All inputs are finite; a program needn't handle non-finite values.
Results may differ from a plain program's by a relative error of at most 0.0036.
The roundings to bfloat16 on the way count: a program that leaves them out, or rounds other values in their place, can miss the bound.
Values may be sent and summed in bfloat16 or wider, within the bound.
A program may use at most 64 MiB of HBM per device.

v0:
```python
import math
import jax
import jax.numpy as jnp
from jax import lax
from jax.sharding import PartitionSpec as P

MX = 4
MY = 4
MZ = 2
highest = lax.Precision.HIGHEST
root_half = 0.7071067811865476
inv_root_two_pi = 0.3989422804014327


def phase_table(mode_ids, cell_ids, length, direction):
    product = mode_ids[:, None] * cell_ids[None, :] % length
    angle = product.astype(jnp.float32) * (2.0 * math.pi / length)
    return (jnp.cos(angle), direction * jnp.sin(angle))


def mode_lists():
    kx_ids = jnp.arange(MX, dtype=jnp.int32) - MX // 2
    ky_ids = jnp.arange(MY, dtype=jnp.int32) - MY // 2
    kz_ids = jnp.arange(MZ, dtype=jnp.int32)
    return (kx_ids, ky_ids, kz_ids)


def complex_contract(real_part, imag_part, cos_t, sin_t, form):

    def product(left, right):
        return jnp.einsum(form, left, right, precision=highest)

    return (
        product(real_part, cos_t) - product(imag_part, sin_t),
        product(real_part, sin_t) + product(imag_part, cos_t),
    )


def forward_modes(grid_field, x_cells, scale):
    grid_len = grid_field.shape[1]
    kx_ids, ky_ids, kz_ids = mode_lists()
    cells = jnp.arange(grid_len, dtype=jnp.int32)
    cos_z, sin_z = phase_table(kz_ids, cells, grid_len, -1.0)
    part_re = jnp.einsum(
        "abzc,kz->abkc", grid_field, cos_z.astype(jnp.bfloat16), preferred_element_type=jnp.float32
    )
    part_im = jnp.einsum(
        "abzc,kz->abkc", grid_field, sin_z.astype(jnp.bfloat16), preferred_element_type=jnp.float32
    )
    cos_y, sin_y = phase_table(ky_ids, cells, grid_len, -1.0)
    next_re, next_im = complex_contract(part_re, part_im, cos_y, sin_y, "abkc,jb->ajkc")
    cos_x, sin_x = phase_table(kx_ids, x_cells, grid_len, -1.0)
    last_re, last_im = complex_contract(next_re, next_im, cos_x, sin_x, "ajkc,ia->ijkc")
    stacked = jnp.stack([last_re, last_im], axis=3) * scale
    return stacked.reshape(MX * MY * MZ, 2, stacked.shape[-1])


def inverse_modes(spectrum, x_cells, grid_len):
    kx_ids, ky_ids, kz_ids = mode_lists()
    cells = jnp.arange(grid_len, dtype=jnp.int32)
    values = spectrum.astype(jnp.float32).reshape(MX, MY, MZ, 2, spectrum.shape[-1])
    cos_x, sin_x = phase_table(kx_ids, x_cells, grid_len, 1.0)
    first_re, first_im = complex_contract(
        values[:, :, :, 0], values[:, :, :, 1], cos_x, sin_x, "ijkc,ia->ajkc"
    )
    cos_y, sin_y = phase_table(ky_ids, cells, grid_len, 1.0)
    second_re, second_im = complex_contract(first_re, first_im, cos_y, sin_y, "ajkc,jb->abkc")
    cos_z, sin_z = phase_table(kz_ids, cells, grid_len, 1.0)
    real_out = jnp.einsum("abkc,kz->abzc", second_re, cos_z, precision=highest)
    real_out = real_out - jnp.einsum("abkc,kz->abzc", second_im, sin_z, precision=highest)
    return real_out * float(MX * MY * MZ) ** (-0.5)


def mix_modes(coeff_b, weights):
    signs = jnp.array([1.0, -1.0], jnp.bfloat16).reshape(1, 2, 1, 1)
    spec_re = jnp.einsum(
        "gmri,mrio->gmo", coeff_b, weights * signs, preferred_element_type=jnp.float32
    )
    spec_im = jnp.einsum(
        "gmri,mrio->gmo", coeff_b[:, :, ::-1], weights, preferred_element_type=jnp.float32
    )
    return jnp.stack([spec_re, spec_im], axis=2)


def weight_grad(coeff_b, back_stack):
    coeff_f = coeff_b.astype(jnp.float32)
    rotated = jnp.stack([-coeff_f[:, :, 1], coeff_f[:, :, 0]], axis=2)
    grad_re = jnp.einsum("gmri,gmro->mio", coeff_f, back_stack, precision=highest)
    grad_im = jnp.einsum("gmri,gmro->mio", rotated, back_stack, precision=highest)
    return jnp.stack([grad_re, grad_im], axis=1)


def point_part(grid_field, branch, local_w, proj, grid_target, scale):
    width = grid_field.shape[-1]
    flat_field = grid_field.reshape(-1, width)
    pre = branch.reshape(-1, width) + jnp.dot(
        flat_field, local_w, preferred_element_type=jnp.float32
    )
    erf_part = lax.erf(pre * root_half)
    active = 0.5 * pre * (1.0 + erf_part)
    pred = jnp.dot(active, proj, precision=highest)
    resid = (pred - grid_target.reshape(-1).astype(jnp.float32)) * scale
    slope = 0.5 * (1.0 + erf_part) + pre * jnp.exp(-0.5 * pre * pre) * inv_root_two_pi
    d_pre = (resid[:, None] * proj[None, :] * slope).astype(jnp.bfloat16)
    local_grad = lax.dot_general(
        flat_field, d_pre, (((0,), (0,)), ((), ())), preferred_element_type=jnp.float32
    )
    return (d_pre.reshape(grid_field.shape), local_grad)


def body(fields, targets, lists, counts, spectral_w, local_w, proj):
    grid_store = fields[0]
    target_store = targets[0]
    slot_order = lists[0]
    slot_count = grid_store.shape[0]
    plane_count = grid_store.shape[1]
    grid_len = grid_store.shape[2]
    width = grid_store.shape[-1]
    lane_index = lax.axis_index("dp")
    x_cells = lax.axis_index("fsdp") * plane_count + jnp.arange(plane_count, dtype=jnp.int32)
    scale = 1.0 / jnp.sum(counts).astype(jnp.float32)
    mode_scale = float(MX * MY * MZ) ** (-0.5)
    full_weights = lax.all_gather(spectral_w, "fsdp", axis=0, tiled=True)
    live_count = counts[lane_index]
    coeff_init = jnp.zeros((slot_count, MX * MY * MZ, 2, width), jnp.float32)

    def forward_pass(position, coeff_stack):
        slot_index = slot_order[position]
        grid_field = lax.dynamic_index_in_dim(grid_store, slot_index, 0, keepdims=False)
        grid_coeff = forward_modes(grid_field, x_cells, float(grid_len) ** (-1.5))
        return lax.dynamic_update_index_in_dim(coeff_stack, grid_coeff, position, 0)

    coeff_stack = lax.fori_loop(0, live_count, forward_pass, coeff_init)
    full_coeff = lax.psum(coeff_stack, "fsdp")
    coeff_b = full_coeff.astype(jnp.bfloat16)
    spectrum = mix_modes(coeff_b, full_weights).astype(jnp.bfloat16)

    def backward_pass(position, carry):
        back_stack, local_total = carry
        slot_index = slot_order[position]
        grid_field = lax.dynamic_index_in_dim(grid_store, slot_index, 0, keepdims=False)
        grid_target = lax.dynamic_index_in_dim(target_store, slot_index, 0, keepdims=False)
        grid_spectrum = lax.dynamic_index_in_dim(spectrum, position, 0, keepdims=False)
        branch = inverse_modes(grid_spectrum, x_cells, grid_len)
        d_pre, local_grad = point_part(grid_field, branch, local_w, proj, grid_target, scale)
        grid_back = forward_modes(d_pre, x_cells, mode_scale)
        return (
            lax.dynamic_update_index_in_dim(back_stack, grid_back, position, 0),
            local_total + local_grad,
        )

    back_init = (jnp.zeros_like(coeff_init), jnp.zeros((width, width), jnp.float32))
    back_stack, local_total = lax.fori_loop(0, live_count, backward_pass, back_init)
    grad_part = lax.psum_scatter(
        weight_grad(coeff_b, back_stack), "fsdp", scatter_dimension=0, tiled=True
    )
    grad_spectral = lax.psum(grad_part, "dp")
    grad_local = lax.psum(local_total, ("dp", "fsdp"))
    return (grad_spectral, grad_local)


def solution(mesh):
    return jax.shard_map(
        body,
        mesh=mesh,
        in_specs=(
            P("dp", None, "fsdp", None, None, None),
            P("dp", None, "fsdp", None),
            P("dp", None),
            P(),
            P("fsdp", None, None, None),
            P(),
            P(),
        ),
        out_specs=(P("fsdp", None, None, None), P()),
        check_vma=False,
    )
```

profile of v0, /device:TPU:1, one launch (start us, length us, event | category | flops | bytes accessed | tf_op | source)
XLA Modules:
  0.0 955.1 jit_solution(6195922219674476142)
XLA Ops:
  7.2 0.7 all-gather.2.cloned.1.call-update
  7.9 1.2 dynamic_slice.42
  9.2 11.0 %while.28 = (s32[]{:T(128)}, f32[6,32,2,128]{3,0,2,1:T(8,128)S(1)}, s32[]{:T(128)}, s32[6]{0:T(128)}, bf16[6,3,48,48,128]{4,3,2,1,0:T(8,128)(2,1)}, /*index=5*/s32[]{:T(128)}, s32[]{:T(128)}, s32[]{:T(128)}, s32[]{:T(128)}) while((s32[]{:T(128)}, f32[6,32,2,128]{3,0,2,1:T(8,128)S(1)}, s32[]{:T(128)}, s32[6]{0:T(128)}, ...), condition=%wide.region_1.2_spmd.clone, body=%wide.region_0.0_spmd.clone.sunk | while | flops 14786103 | bytes 4907401 | solution.py:133
  9.9 1.3 dynamic_slice.73
  13.2 1.9 fusion.419
  15.4 1.9 fusion.421
  17.3 0.3 fusion.422
  18.2 0.3 fusion.425
  20.3 0.7 reduce_sum.9
  21.0 70.4 %all-reduce.11 = bf16[6,32,2,128]{3,0,2,1:T(8,128)(2,1)S(1)} all-reduce(f32[6,32,2,128]{3,0,2,1:T(8,128)S(1)} %get-tuple-element.239), channel_id=1, replica_groups=mesh['dp'=16,'fsdp'=16] {'fsdp'}, use_global_device_ids=true, to_apply=%region_2.3 | all-reduce | flops 49152 | bytes 294912 | tf_op jit(solution)/shard_map/psum | solution.py:134
  92.3 5.5 all-gather.2.cloned.1.call-done
  97.7 2.0 fusion.287
  99.7 2.0 fusion.288
  101.9 34.5 %while.29 = (s32[]{:T(128)}, f32[6,32,2,128]{3,0,2,1:T(8,128)S(1)}, f32[128,128]{1,0:T(8,128)S(1)}, s32[]{:T(128)}, bf16[6,32,2,128]{3,1,2,0:T(8,128)(2,1)S(1)},...) while((s32[]{:T(128)}, f32[6,32,2,128]{3,0,2,1:T(8,128)S(1)}, ...), condition=%wide.region_5.6_spmd.clone, body=%wide.region_4.5_spmd.clone.sunk | while | flops 544574080 | bytes 70409384 | solution.py:153
  102.8 0.3 fusion.470
  103.2 0.3 convolution_subtract_fusion.10
  103.5 0.5 fusion.471
  104.0 0.3 fusion.472
  104.3 0.3 convolution_add_fusion.14
  104.7 0.5 fusion.473
  105.1 3.1 fusion.474
  108.2 0.5 fusion.475
  108.7 0.5 fusion.476
  109.2 5.0 subtract_multiply_fusion.4
  114.2 0.7 dynamic_slice.77
  116.9 1.9 constant_dynamic-slice_fusion.6
  118.8 0.6 copy-done
  119.4 0.6 convolution_add_fusion.15
  120.1 1.7 copy-done.1
  121.8 3.7 fusion.477
  125.5 0.7 dynamic-slice_convert_fusion.2
  126.2 5.2 fusion.478
  131.4 0.7 convolution_add_fusion.17
  132.1 0.4 convolution_bitcast_fusion.7
  132.8 0.4 convolution_bitcast_fusion.8
  133.8 0.3 fusion.480
  136.4 1.0 convolution_bitcast_fusion.3
  137.5 3.5 convolution_bitcast_fusion.2
  140.9 2.2 pad_maximum_fusion
  143.3 0.6 copy-done.7
  143.9 0.6 dynamic-slice
  145.1 423.9 %all-reduce.10.cloned.1.call-done = f32[32,2,128,128]{3,2,0,1:T(8,128)} async-done(((f32[32,2,128,128]{3,2,0,1:T(8,128)}), f32[32,2,128,128]{3,2,0,1:T(8,128)}) %all-reduce.10.cloned.1.call-update) | async-done | bytes 4194320
  569.0 1.7 constant_dynamic-slice_fusion.2
  570.7 0.5 all-reduce.8.cloned.1.call-update
  571.3 127.2 %all-reduce.6.cloned.1.call-done = f32[2,2,128,128]{3,2,0,1:T(8,128)} async-done(((f32[2,2,128,128]{3,2,0,1:T(8,128)}), f32[2,2,128,128]{3,2,0,1:T(8,128)}) %all-reduce.6.cloned.1.call-update) | async-done | bytes 262160 | tf_op jit(solution)/shard_map/psum | solution.py:157
  698.5 1.7 copy.102
  700.1 246.9 %all-reduce.8.cloned.1.call-done = f32[128,128]{1,0:T(8,128)} async-done(((f32[128,128]{1,0:T(8,128)}), f32[128,128]{1,0:T(8,128)}) %all-reduce.8.cloned.1.call-update) | async-done | bytes 65552 | tf_op jit(solution)/shard_map/psum | solution.py:158
  947.1 1.5 copy.274
  (61 shorter events, 4.6 us)
Async XLA Ops:
  7.2 90.6 %all-gather.2.cloned.1.call-start = ((), (), s32[]{:S(2)}) async-start(), calls=%async_computation | async-start | bytes 2228224 | tf_op jit(solution)/shard_map/all_gather | solution.py:123
  7.9 561.1 %all-reduce.10.cloned.1.call-start = ((), (), s32[]{:S(2)}) async-start(), calls=%async_computation.3 | async-start | bytes 8388608
  9.2 11.1 %copy-start.5 = (s32[16]{0:T(128)S(1)}, s32[16]{0:T(128)}, u32[]{:S(2)}) copy-start(s32[16]{0:T(128)} %param.15) | copy-start | bytes 196
  20.3 79.5 %copy-start.8 = (bf16[2]{0:T(256)(128)(2,1)S(1)}, bf16[2]{0:T(256)(128)(2,1)}, u32[]{:S(2)}) copy-start(bf16[2]{0:T(256)(128)(2,1)} %constant.200.clone) | copy-start | bytes 16
  91.5 10.5 %copy-start.3 = (bf16[128,128]{1,0:T(8,128)(2,1)S(1)}, bf16[128,128]{1,0:T(8,128)(2,1)}, u32[]{:S(2)}) copy-start(bf16[128,128]{1,0:T(8,128)(2,1)} %param.17) | copy-start | bytes 98308
  91.5 10.4 %copy-start.4 = (f32[128]{0:T(128)S(1)}, f32[128]{0:T(128)}, u32[]{:S(2)}) copy-start(f32[128]{0:T(128)} %param.18) | copy-start | bytes 1540
  91.5 10.4 %copy-start.6 = (s32[6]{0:T(128)S(1)}, s32[6]{0:T(128)}, u32[]{:S(2)}) copy-start(s32[6]{0:T(128)} %get-tuple-element.573) | copy-start | bytes 76
  116.9 2.5 copy-start
  120.0 1.7 copy-start.1
  136.4 6.8 copy-start.2
  143.2 0.7 copy-start.7
  143.2 555.3 %all-reduce.6.cloned.1.call-start = ((), (), s32[]{:S(2)}) async-start(), calls=%async_computation.1 | async-start | bytes 524288 | tf_op jit(solution)/shard_map/psum | solution.py:157
  570.7 376.4 %all-reduce.8.cloned.1.call-start = ((), (), s32[]{:S(2)}) async-start(), calls=%async_computation.2 | async-start | bytes 131072 | tf_op jit(solution)/shard_map/psum | solution.py:158
Sparse Core Ops, SparseCore 0:
  10.6 87.1 all-gather.1
  143.3 425.6 all-reduce.9
  572.2 126.2 all-reduce.5
  704.4 242.6 all-reduce.7
where the time goes:
time: 957 us; the launch traced here: 955 us
  waiting for transfers between devices  805 us (84%)
  blocking collectives  70.4 us (7%)
  matrix products  33.9 us (4%)
  between operations  15.3 us (2%)
  local copies, waits for them, and re-layouts  14 us (1%)
    unnamed x5, waiting for transfers between devices  425 us
    psum x1, waiting for transfers between devices, body(): grad_local = lax.psum(local_total, ('dp', 'fsdp'))  247 us
    psum x1, waiting for transfers between devices, body(): grad_spectral = lax.psum(grad_part, 'dp')  127 us
    psum x1, blocking collectives, body(): full_coeff = lax.psum(coeff_stack, 'fsdp')  70.4 us
  transfers between devices with their start and end apart: 4, of which 4 were waited for; matrix products, arithmetic and copies ran while one was open for 1% of the time, Pallas kernels for 0%

commit v1 on v0

--- a/solution.py
+++ b/solution.py
@@ -154,7 +154,7 @@
     grad_part = lax.psum_scatter(
         weight_grad(coeff_b, back_stack), "fsdp", scatter_dimension=0, tiled=True
     )
-    grad_spectral = lax.psum(grad_part, "dp")
+    grad_spectral = jnp.sum(lax.all_gather(grad_part, "dp"), axis=0)
     grad_local = lax.psum(local_total, ("dp", "fsdp"))
     return (grad_spectral, grad_local)
 

time: 957 us -> 872 us (0.911)
  waiting for transfers between devices: 805 us -> 718 us
    psum x1 -> x0, waiting for transfers between devices: 127 us -> none  [body(): grad_spectral = lax.psum(grad_part, 'dp')]
    all_gather x0 -> x1, waiting for transfers between devices: none -> 43.5 us  [body(): grad_spectral = jnp.sum(lax.all_gather(grad_part, 'dp'), axis=0)]
  transfers between devices with their start and end apart: 4 -> 4, of which waited for: 4 -> 4; matrix products, arithmetic and copies ran while one was open for 1% -> 2% of each run, Pallas kernels for 0% -> 0%
where the time goes in v1:
time: 872 us; the launch traced here: 870 us
  waiting for transfers between devices  718 us (82%)
  blocking collectives  70.4 us (8%)
  matrix products  33.9 us (4%)
  between operations  15.3 us (2%)
  local copies, waits for them, and re-layouts  13.1 us (2%)
  other arithmetic  11.4 us (1%)
    unnamed x5, waiting for transfers between devices  425 us
    psum x1, waiting for transfers between devices, body(): grad_local = lax.psum(local_total, ('dp', 'fsdp'))  244 us
    psum x1, blocking collectives, body(): full_coeff = lax.psum(coeff_stack, 'fsdp')  70.4 us
    all_gather x1, waiting for transfers between devices, body(): grad_spectral = jnp.sum(lax.all_gather(grad_part, 'dp'), axis=0)  43.5 us
  transfers between devices with their start and end apart: 4, of which 4 were waited for; matrix products, arithmetic and copies ran while one was open for 2% of the time, Pallas kernels for 0%

profile of v1, /device:TPU:1, one launch (start us, length us, event | category | flops | bytes accessed | tf_op | source)
XLA Modules:
  0.0 870.2 jit_solution(8463158561614833300)
XLA Ops:
  7.2 0.7 all-gather.4.cloned.1.call-update
  7.9 1.2 dynamic_slice.42
  9.2 11.0 %while.28 = (s32[]{:T(128)}, f32[6,32,2,128]{3,0,2,1:T(8,128)S(1)}, s32[]{:T(128)}, s32[6]{0:T(128)}, bf16[6,3,48,48,128]{4,3,2,1,0:T(8,128)(2,1)}, /*index=5*/s32[]{:T(128)}, s32[]{:T(128)}, s32[]{:T(128)}, s32[]{:T(128)}) while((s32[]{:T(128)}, f32[6,32,2,128]{3,0,2,1:T(8,128)S(1)}, s32[]{:T(128)}, s32[6]{0:T(128)}, ...), condition=%wide.region_1.2_spmd.clone, body=%wide.region_0.0_spmd.clone.sunk | while | flops 14786103 | bytes 4907401 | solution.py:133
  9.9 1.3 dynamic_slice.73
  13.2 1.9 fusion.419
  15.4 1.9 fusion.421
  18.2 0.3 fusion.425
  20.3 0.7 reduce_sum.18
  21.0 70.4 %all-reduce.8 = bf16[6,32,2,128]{3,0,2,1:T(8,128)(2,1)S(1)} all-reduce(f32[6,32,2,128]{3,0,2,1:T(8,128)S(1)} %get-tuple-element.239), channel_id=1, replica_groups=mesh['dp'=16,'fsdp'=16] {'fsdp'}, use_global_device_ids=true, to_apply=%region_2.3 | all-reduce | flops 49152 | bytes 294912 | tf_op jit(solution)/shard_map/psum | solution.py:134
  92.3 5.5 all-gather.4.cloned.1.call-done
  97.7 2.0 fusion.287
  99.7 2.0 fusion.288
  101.9 34.5 %while.29 = (s32[]{:T(128)}, f32[6,32,2,128]{3,0,2,1:T(8,128)S(1)}, f32[128,128]{1,0:T(8,128)S(1)}, s32[]{:T(128)}, bf16[6,32,2,128]{3,1,2,0:T(8,128)(2,1)S(1)},...) while((s32[]{:T(128)}, f32[6,32,2,128]{3,0,2,1:T(8,128)S(1)}, ...), condition=%wide.region_5.6_spmd.clone, body=%wide.region_4.5_spmd.clone.sunk | while | flops 544574080 | bytes 70409384 | solution.py:153
  102.8 0.3 fusion.470
  103.2 0.3 convolution_subtract_fusion.10
  103.5 0.5 fusion.471
  104.0 0.3 fusion.472
  104.3 0.3 convolution_add_fusion.14
  104.7 0.5 fusion.473
  105.1 3.1 fusion.474
  108.2 0.5 fusion.475
  108.7 0.5 fusion.476
  109.2 5.0 subtract_multiply_fusion.4
  114.2 0.7 dynamic_slice.77
  116.9 1.9 constant_dynamic-slice_fusion.6
  118.8 0.6 copy-done
  119.4 0.6 convolution_add_fusion.15
  120.1 1.7 copy-done.1
  121.8 3.7 fusion.477
  125.5 0.7 dynamic-slice_convert_fusion.2
  126.3 5.2 fusion.478
  131.5 0.7 convolution_add_fusion.17
  132.1 0.4 convolution_bitcast_fusion.7
  132.8 0.4 convolution_bitcast_fusion.8
  133.8 0.3 fusion.480
  136.4 1.0 convolution_bitcast_fusion.3
  137.5 3.5 convolution_bitcast_fusion.2
  140.9 2.2 pad_maximum_fusion
  143.3 0.6 copy-done.7
  143.9 0.6 dynamic-slice
  145.1 423.9 %all-reduce.7.cloned.1.call-done = f32[32,2,128,128]{3,2,0,1:T(8,128)} async-done(((f32[32,2,128,128]{3,2,0,1:T(8,128)}), f32[32,2,128,128]{3,2,0,1:T(8,128)}) %all-reduce.7.cloned.1.call-update) | async-done | bytes 4194320
  569.0 1.7 constant_dynamic-slice_fusion.2
  570.8 0.5 all-reduce.5.cloned.1.call-update
  571.3 43.5 %all-gather.6.cloned.1.call-done = f32[32,2,128,128]{3,2,0,1:T(8,128)} async-done(((f32[2,2,128,128]{3,2,0,1:T(8,128)}), f32[32,2,128,128]{3,2,0,1:T(8,128)}) %all-gather.6.cloned.1.call-update) | async-done | bytes 4194320 | tf_op jit(solution)/shard_map/all_gather | solution.py:157
  614.8 2.4 reduce_sum.19
  617.2 0.7 copy.100
  617.9 244.3 %all-reduce.5.cloned.1.call-done = f32[128,128]{1,0:T(8,128)} async-done(((f32[128,128]{1,0:T(8,128)}), f32[128,128]{1,0:T(8,128)}) %all-reduce.5.cloned.1.call-update) | async-done | bytes 65552 | tf_op jit(solution)/shard_map/psum | solution.py:158
  862.2 1.5 copy.273
  (62 shorter events, 4.9 us)
Async XLA Ops:
  7.2 90.6 %all-gather.4.cloned.1.call-start = ((), (), s32[]{:S(2)}) async-start(), calls=%async_computation | async-start | bytes 2228224 | tf_op jit(solution)/shard_map/all_gather | solution.py:123
  7.9 561.1 %all-reduce.7.cloned.1.call-start = ((), (), s32[]{:S(2)}) async-start(), calls=%async_computation.3 | async-start | bytes 8388608
  9.2 11.1 %copy-start.5 = (s32[16]{0:T(128)S(1)}, s32[16]{0:T(128)}, u32[]{:S(2)}) copy-start(s32[16]{0:T(128)} %param.15) | copy-start | bytes 196
  20.3 79.5 %copy-start.8 = (bf16[2]{0:T(256)(128)(2,1)S(1)}, bf16[2]{0:T(256)(128)(2,1)}, u32[]{:S(2)}) copy-start(bf16[2]{0:T(256)(128)(2,1)} %constant.201.clone) | copy-start | bytes 16
  91.5 10.5 %copy-start.3 = (bf16[128,128]{1,0:T(8,128)(2,1)S(1)}, bf16[128,128]{1,0:T(8,128)(2,1)}, u32[]{:S(2)}) copy-start(bf16[128,128]{1,0:T(8,128)(2,1)} %param.17) | copy-start | bytes 98308
  91.5 10.4 %copy-start.4 = (f32[128]{0:T(128)S(1)}, f32[128]{0:T(128)}, u32[]{:S(2)}) copy-start(f32[128]{0:T(128)} %param.18) | copy-start | bytes 1540
  91.5 10.4 %copy-start.6 = (s32[6]{0:T(128)S(1)}, s32[6]{0:T(128)}, u32[]{:S(2)}) copy-start(s32[6]{0:T(128)} %get-tuple-element.569) | copy-start | bytes 76
  116.9 2.5 copy-start
  120.1 1.7 copy-start.1
  136.4 6.8 copy-start.2
  143.2 0.7 copy-start.7
  143.2 471.6 %all-gather.6.cloned.1.call-start = ((), (), s32[]{:S(2)}) async-start(), calls=%async_computation.2 | async-start | bytes 4456448 | tf_op jit(solution)/shard_map/all_gather | solution.py:157
  570.7 291.5 %all-reduce.5.cloned.1.call-start = ((), (), s32[]{:S(2)}) async-start(), calls=%async_computation.1 | async-start | bytes 131072 | tf_op jit(solution)/shard_map/psum | solution.py:158
Sparse Core Ops, SparseCore 0:
  10.6 87.1 all-gather.3
  143.3 425.6 all-reduce.6
  571.4 43.3 all-gather.5
  620.7 241.4 all-reduce.4
